TPU v7x, 32 devices: a whole 2x2x4 slice. The times are simulated.
32 devices in a mesh: parts: 2 (over y), seq: 4 (over z), head: 4 (over x, core).
Axes of the slice: x: 2, y: 2, z: 4, core: 2. Of those that a mesh axis runs over, the one named last changes fastest.
Arguments:
- hidden: bfloat16 [48, 12288], P(('parts', 'head'), 'seq'), parts along dimension 0, may hold values from -600 to 600
- norm_gain: float32 [12288], P('seq'), may hold values from 0.1 to 1.9
- w_query: bfloat16 [12288, 12288], P('seq', 'head'), may hold values from -0.0546875 to 0.0546875
- w_key: bfloat16 [12288, 1024], P('seq', 'head'), may hold values from -0.0546875 to 0.0546875
- w_value: bfloat16 [12288, 1024], P('seq', 'head'), may hold values from -0.0546875 to 0.0546875
- w_out: bfloat16 [12288, 12288], P('head', 'seq'), may hold values from -0.0546875 to 0.0546875
- lengths: int32 [48], P('parts'), parts along dimension 0, may hold values from 1 to 512, as said below
- key_cache: bfloat16 [48, 8, 512, 128], P('parts', 'head', 'seq'), parts along dimension 0, may hold values from -600 to 600, as said below
- value_cache: bfloat16 [48, 8, 512, 128], P('parts', 'head', 'seq'), parts along dimension 0, may hold values from -6 to 6
Outputs:
- attn_out: bfloat16 [48, 12288], P(('parts', 'head'), 'seq'), parts along dimension 0
There are 2 independent parts, one for each index of `parts`. A program takes and returns all parts, laid end to end along the dimension named above; an argument that names none is the same for every part. Nothing has to cross between parts.
Inputs may be any that keep to these rules, and one draw needn't show every extreme that they name: Sequence b holds lengths[b] cached tokens at positions 0 to lengths[b] - 1; its new token takes position lengths[b]. `key_cache`: positions at or past a sequence's length hold no data.
All inputs are finite; a program needn't handle non-finite values.
Results may differ from a plain program's by a relative error of at most 0.0075.
The roundings to bfloat16 on the way count: a program that leaves them out, or rounds other values in their place, can miss the bound.
Values may be sent and summed in bfloat16 or wider, within the bound.
A program may use at most 128 MiB of HBM per device.

v0:
```python
import jax
import jax.numpy as jnp
from jax import lax
from jax.sharding import PartitionSpec as P

D = 12288
EPSILON = 1e-05


def joined(value, axis, join):
    pieces = jax.tree.map(lambda part: lax.all_gather(part, axis), value)
    head = jax.tree.map(lambda part: part[0], pieces)
    tail = jax.tree.map(lambda part: part[1:], pieces)
    subtotal, _ = lax.scan(lambda subtotal, slab: (join(subtotal, slab), None), head, tail)
    return subtotal


def join_parts(earlier, later):
    new_max = jnp.maximum(earlier[0], later[0])
    left_factor = jnp.exp(earlier[0] - new_max)
    right_factor = jnp.exp(later[0] - new_max)
    den_total = earlier[1] * left_factor + later[1] * right_factor
    acc_total = earlier[2] * left_factor[..., None] + later[2] * right_factor[..., None]
    return (new_max, den_total, acc_total)


def local(hidden, norm_gain, w_query, w_key, w_value, w_out, lengths, key_cache, value_cache):
    batch_size, kv_local, block_len, head_size = key_cache.shape
    group_size = w_query.shape[1] // (kv_local * head_size)
    token_rows = lax.all_gather(hidden, "head", axis=0, tiled=True)
    widened = token_rows.astype(jnp.float32)
    square_local = jnp.sum(widened * widened, axis=1)
    scaled = (widened * norm_gain).astype(jnp.bfloat16)
    query_part = jnp.dot(scaled, w_query, preferred_element_type=jnp.float32)
    key_part = jnp.dot(scaled, w_key, preferred_element_type=jnp.float32)
    value_part = jnp.dot(scaled, w_value, preferred_element_type=jnp.float32)
    query_factor = float(head_size) ** (-0.5)
    norm_total = lax.psum(square_local, "seq")
    query_sum, key_sum, value_sum = lax.psum((query_part, key_part, value_part), "seq")
    inverse_rms = lax.rsqrt(norm_total / D + EPSILON)[:, None]
    queries = (query_sum * inverse_rms * query_factor).astype(jnp.bfloat16)
    new_keys = (key_sum * inverse_rms).astype(jnp.bfloat16)
    new_values = (value_sum * inverse_rms).astype(jnp.bfloat16)
    grouped = queries.reshape(batch_size, kv_local, group_size, head_size)
    scores = jnp.einsum("bkgd,bkpd->bkgp", grouped, key_cache, preferred_element_type=jnp.float32)
    offset = lax.axis_index("seq") * block_len
    positions = offset + jnp.arange(block_len, dtype=jnp.int32)
    live_mask = (positions[None, :] < lengths[:, None])[:, None, None, :]
    block_max = jnp.max(jnp.where(live_mask, scores, -1e30), axis=-1)
    shifted = jnp.where(live_mask, scores - block_max[..., None], 0.0)
    weights = jnp.where(live_mask, jnp.exp(shifted), 0.0).astype(jnp.bfloat16)
    block_den = jnp.sum(weights.astype(jnp.float32), axis=-1)
    block_acc = jnp.einsum(
        "bkgp,bkpd->bkgd", weights, value_cache, preferred_element_type=jnp.float32
    )
    self_score = jnp.einsum(
        "oips,ois->oip",
        grouped,
        new_keys.reshape(batch_size, kv_local, head_size),
        preferred_element_type=jnp.float32,
    )
    global_max, den_merged, acc_merged = joined(
        (block_max, block_den, block_acc), "seq", join_parts
    )
    top_score = jnp.maximum(global_max, self_score)
    factors = jnp.exp(global_max - top_score)
    den_sum = den_merged * factors
    acc_sum = acc_merged * factors[..., None]
    own_weight = jnp.exp(self_score - top_score)
    denominator = den_sum + own_weight
    numerator = acc_sum + own_weight[..., None] * new_values.reshape(
        batch_size, kv_local, 1, head_size
    ).astype(jnp.float32)
    mixed = (
        (numerator / denominator[..., None])
        .astype(jnp.bfloat16)
        .reshape(batch_size, kv_local * group_size * head_size)
    )
    output = lax.psum_scatter(
        jnp.dot(mixed, w_out, preferred_element_type=jnp.float32),
        "head",
        scatter_dimension=0,
        tiled=True,
    )
    return output.astype(jnp.bfloat16)


def solution(mesh):
    return jax.shard_map(
        local,
        mesh=mesh,
        in_specs=(
            P(("parts", "head"), "seq"),
            P("seq"),
            P("seq", "head"),
            P("seq", "head"),
            P("seq", "head"),
            P("head", "seq"),
            P("parts"),
            P("parts", "head", "seq", None),
            P("parts", "head", "seq", None),
        ),
        out_specs=P(("parts", "head"), "seq"),
        check_vma=False,
    )
```

profile of v0, /device:TPU:1, one launch (start us, length us, event | category | flops | bytes accessed | tf_op | source)
XLA Modules:
  0.0 132.5 jit_solution(6576906076258920298)
XLA Ops:
  6.5 7.0 %all-gather.3 = bf16[4,6,3072]{2,1,0:T(8,128)(2,1)S(1)} all-gather(bf16[1,6,3072]{2,1,0:T(8,128)(2,1)} %bitcast.49), channel_id=1, replica_groups=mesh['parts'=2,'seq'=4,'head'=4] {'head'}, dimensions={0}, use_global_device_ids=true | all-gather | bytes 184320 | tf_op jit(solution)/shard_map/all_gather | solution.py:30
  13.6 0.9 multiply_reduce_fusion
  14.5 9.8 %fusion.12 = f32[24,3072]{1,0:T(8,128)} fusion(bf16[24,3072]{1,0:T(8,128)(2,1)S(1)} %get-tuple-element.86, bf16[3072,3072]{1,0:T(8,128)(2,1)} %param.13), kind=kOutput, calls=%fused_computation.30 | convolution fusion | flops 452984832 | bytes 19316736 | tf_op jit(solution)/shard_map/dot_general | solution.py:34
  24.7 1.1 copy-done.2
  26.1 17.1 %all-reduce.2 = (f32[24]{0:T(128)S(1)}, f32[24,256]{1,0:T(8,128)S(1)}, f32[24,256]{1,0:T(8,128)S(1)}) all-reduce(f32[24]{0:T(128)S(1)} %get-tuple-element.85, f32[24,256]{1,0:T(8,128)S(1)} %fusion.13, f32[24,256]{1,0:T(8,128)S(1)} %fusion.15), channel_id=1, replica_groups=mesh['parts'=2,'seq'=4,'head'=4] {'seq'}, use_global_device_ids=true, to_apply=%region_2.0 | all-reduce | flops 12312 | bytes 98496 | tf_op jit(solution)/shard_map/psum | solution.py:38
  43.3 16.5 %all-reduce.5.cloned.1.call-done = f32[24,3072]{1,0:T(8,128)} async-done(((f32[24,3072]{1,0:T(8,128)}), f32[24,3072]{1,0:T(8,128)}) %all-reduce.5.cloned.1.call-update) | async-done | bytes 294928 | tf_op jit(solution)/shard_map/psum | solution.py:39
  59.8 1.1 multiply_convert_fusion
  61.0 1.0 select_reduce_fusion
  62.0 2.0 %fusion.8 = f32[24,2,12,128]{3,2,1,0:T(8,128)S(1)} fusion(bf16[24,2,128,128]{3,2,1,0:T(8,128)(2,1)} %param.19, f32[24,2,12,128]{3,2,1,0:T(8,128)S(1)} %get-tuple-element.90, f32[24,2,12]{2,1,0:T(2,128)S(1)} %get-tuple-element.89, pred[24,128]{1,0:T(8,128)(4,1)S(1)} %broadcast_compare_fusion), kind=kOutput, calls=%fused_computation.29 | convolution fusion | flops 19169280 | bytes 2168064 | tf_op jit(solution)/shard_map/bkgp,bkpd->bkgd/dot_general | solution.py:53
  64.0 0.9 copy.26
  65.0 10.4 %all-gather = f32[96,2,12]{2,1,0:T(2,128)S(1)} all-gather(f32[24,2,12]{2,1,0:T(2,128)S(1)} %get-tuple-element.89), channel_id=2, replica_groups=mesh['parts'=2,'seq'=4,'head'=4] {'seq'}, dimensions={0}, use_global_device_ids=true | all-gather | bytes 11520 | tf_op jit(solution)/shard_map/all_gather | solution.py:11
  75.8 11.5 %all-gather.1 = f32[96,2,12]{2,1,0:T(2,128)S(1)} all-gather(f32[24,2,12]{2,1,0:T(2,128)S(1)} %convert_reduce_fusion), channel_id=3, replica_groups=mesh['parts'=2,'seq'=4,'head'=4] {'seq'}, dimensions={0}, use_global_device_ids=true | all-gather | bytes 11520 | tf_op jit(solution)/shard_map/all_gather | solution.py:11
  88.0 10.4 %all-gather.6.cloned.1.call-done = f32[96,2,12,128]{3,1,2,0:T(2,128)} async-done(((f32[24,2,12,128]{3,1,2,0:T(2,128)}), f32[96,2,12,128]{3,1,2,0:T(2,128)}) %all-gather.6.cloned.1.call-update) | async-done | bytes 1179664 | tf_op jit(solution)/shard_map/all_gather | solution.py:11
  98.5 1.1 slice.32
  99.7 2.0 %while.14 = (s32[]{:T(128)}, f32[24,2,12]{0,1,2:T(2,128)S(1)}, f32[24,2,12]{0,1,2:T(2,128)S(1)}, f32[24,2,12,128]{3,2,1,0:T(8,128)S(1)}, f32[3,24,2,12]{1,2,3,0:...) while((s32[]{:T(128)}, f32[24,2,12]{0,1,2:T(2,128)S(1)}, ...), condition=%wide.region_6.7_spmd, body=%wide.region_5.6_spmd.sunk | while | flops 224642 | bytes 1506917 | solution.py:14
  100.0 0.4 fusion.33
  100.7 0.4 fusion.33
  101.3 0.4 fusion.33
  102.0 0.4 divide_convert_fusion
  102.5 7.7 %fusion.16 = f32[24,3072]{1,0:T(8,128)S(1)} fusion(bf16[24,3072]{1,0:T(8,128)(2,1)S(1)} %reshape.56, bf16[3072,3072]{1,0:T(8,128)(2,1)} %param.16), kind=kOutput, calls=%fused_computation.34 | convolution fusion | flops 452984832 | bytes 19316736 | tf_op jit(solution)/shard_map/dot_general | solution.py:80
  110.2 9.0 %fusion = f32[8,3072]{1,0:T(8,128)S(1)} fusion(f32[24,3072]{1,0:T(8,128)S(1)} %fusion.16), kind=kCustom, calls=%all-reduce-scatter | all-reduce-scatter fusion | flops 98305 | bytes 393728
  119.2 4.3 %collective-permute-start = (bf16[6,3072]{1,0:T(8,128)(2,1)S(1)}, bf16[6,3072]{1,0:T(8,128)(2,1)S(1)}, u32[]{:S(2)}, u32[]{:S(2)}) collective-permute-start(bf16[6,3072]{1,0:T(8,128)(2,1)S(1)} %slice.36), channel_id=1, source_target_pairs={{0,1},{1,2},{2,3},{4,5},{5,6},{6,7},{8,9},{9,10},{10,11},{12,13},{... | collective-permute-start | bytes 110600
  123.6 0.6 dynamic-slice.4
  125.0 0.6 dynamic-slice_convert_fusion
  (57 shorter events, 3.8 us)
Async XLA Ops:
  6.5 54.4 %copy-start = (bf16[24,2,128,128]{3,2,1,0:T(8,128)(2,1)S(1)}, bf16[24,2,128,128]{3,2,1,0:T(8,128)(2,1)}, u32[]{:S(2)}) copy-start(bf16[24,2,128,128]{3,2,1,0:T(8,128)(2,1)} %param.18) | copy-start | bytes 4718596
  6.5 53.2 %all-reduce.5.cloned.1.call-start = ((), (), s32[]{:S(2)}) async-start(), calls=%async_computation | async-start | bytes 589824 | tf_op jit(solution)/shard_map/psum | solution.py:39
  14.5 9.8 %copy-start.1 = (bf16[3072,256]{1,0:T(8,128)(2,1)S(1)}, bf16[3072,256]{1,0:T(8,128)(2,1)}, u32[]{:S(2)}) copy-start(bf16[3072,256]{1,0:T(8,128)(2,1)} %param.15) | copy-start | bytes 4718596
  24.3 74.2 %all-gather.6.cloned.1.call-start = ((), (), s32[]{:S(2)}) async-start(), calls=%async_computation.1 | async-start | bytes 1474560 | tf_op jit(solution)/shard_map/all_gather | solution.py:11
  24.3 1.4 %copy-start.2 = (bf16[3072,256]{1,0:T(8,128)(2,1)S(1)}, bf16[3072,256]{1,0:T(8,128)(2,1)}, u32[]{:S(2)}) copy-start(bf16[3072,256]{1,0:T(8,128)(2,1)} %param.14) | copy-start | bytes 4718596
  24.4 18.9 %copy-start.4 = (s32[24]{0:T(128)S(1)}, s32[24]{0:T(128)}, u32[]{:S(2)}) copy-start(s32[24]{0:T(128)} %param.17) | copy-start | bytes 292
  98.5 1.3 slice-start
  102.5 21.0 %copy-start.3 = (u32[32]{0:T(128)S(1)}, u32[32]{0:T(128)}, u32[]{:S(2)}) copy-start(u32[32]{0:T(128)} %constant.37) | copy-start | bytes 388
  119.2 5.6 %collective-permute-start = (bf16[6,3072]{1,0:T(8,128)(2,1)S(1)}, bf16[6,3072]{1,0:T(8,128)(2,1)S(1)}, u32[]{:S(2)}, u32[]{:S(2)}) collective-permute-start(bf16[6,3072]{1,0:T(8,128)(2,1)S(1)} %slice.36), channel_id=1, source_target_pairs={{0,1},{1,2},{2,3},{4,5},{5,6},{6,7},{8,9},{9,10},{10,11},{12,13},{... | collective-permute-start | bytes 110600
Sparse Core Ops, SparseCore 0:
  24.4 35.3 all-reduce.4
  65.0 33.4 all-gather.5
where the time goes:
time: 133 us; the launch traced here: 132 us
  blocking collectives  55.1 us (41%)
  waiting for transfers between devices  26.9 us (20%)
  matrix products  21.3 us (16%)
  between operations  14.3 us (11%)
  local copies, waits for them, and re-layouts  6.41 us (5%)
  starting transfers between devices  4.35 us (3%)
  other arithmetic  4.09 us (3%)
    all_gather x2, blocking collectives, joined(): pieces = jax.tree.map(lambda part: lax.all_gather(part, axis), value)  21.9 us
    psum x1, blocking collectives, local(): norm_total = lax.psum(square_local, 'seq')  17.1 us
    psum x1, waiting for transfers between devices, local(): lax.psum((query_part, key_part, value_part), 'seq')  16.5 us
    all_gather x1, waiting for transfers between devices, joined(): pieces = jax.tree.map(lambda part: lax.all_gather(part, axis), value)  10.4 us
    dot_general x1, matrix products, local(): query_part = jnp.dot(scaled, w_query, preferred_element_type=jnp.float32)  9.76 us
    unnamed x1, blocking collectives  8.98 us
    dot_general x1, matrix products, local(): jnp.dot(mixed, w_out, preferred_element_type=jnp.float32)  7.7 us
    all_gather x1, blocking collectives, local(): token_rows = lax.all_gather(hidden, 'head', axis=0, tiled=True)  7.05 us
  transfers between devices with their start and end apart: 3, of which 2 were waited for; matrix products, arithmetic and copies ran while one was open for 2% of the time, Pallas kernels for 0%

commit v1 on v0

--- a/solution.py
+++ b/solution.py
@@ -1,3 +1,4 @@
+import functools
 import jax
 import jax.numpy as jnp
 from jax import lax
@@ -5,6 +6,17 @@
 
 D = 12288
 EPSILON = 1e-05
+
+
+def serve_the_point(x_part, named_axis):
+    num = lax.axis_size(named_axis)
+    d_next = x_part
+    for k0 in [[(t, t ^ ix) for t in range(num)] for ix in (1, 2, 4, 8, 16) if ix < num]:
+        d_next = d_next + lax.ppermute(d_next, axis_name=named_axis, perm=k0)
+    return d_next
+
+
+use_joints_all = functools.partial(serve_the_point, named_axis="seq")
 
 
 def joined(value, axis, join):
@@ -35,7 +47,7 @@
     key_part = jnp.dot(scaled, w_key, preferred_element_type=jnp.float32)
     value_part = jnp.dot(scaled, w_value, preferred_element_type=jnp.float32)
     query_factor = float(head_size) ** (-0.5)
-    norm_total = lax.psum(square_local, "seq")
+    norm_total = use_joints_all(square_local)
     query_sum, key_sum, value_sum = lax.psum((query_part, key_part, value_part), "seq")
     inverse_rms = lax.rsqrt(norm_total / D + EPSILON)[:, None]
     queries = (query_sum * inverse_rms * query_factor).astype(jnp.bfloat16)

time: 133 us -> 149 us (1.12)
  blocking collectives: 55.1 us -> 63.8 us
  waiting for transfers between devices: 26.9 us -> 31.4 us
  starting transfers between devices: 4.35 us -> 8.29 us
    psum x1, waiting for transfers between devices: 16.5 us -> 30.4 us  [local(): lax.psum((query_part, key_part, value_part), 'seq')]
    all_gather x1, waiting for transfers between devices: 10.4 us -> 0.02 us  [joined(): pieces = jax.tree.map(lambda part: lax.all_gather(part, axis), value)]
    unnamed x1, blocking collectives: 8.98 us -> 18.1 us
    ppermute x0 -> x2, starting transfers between devices: none -> 3.94 us  [serve_the_point(): d_next = d_next + lax.ppermute(d_next, axis_name=named_axis, perm=k0)]
    dot_general x1, matrix products: 0.32 us -> 1.84 us  [local(): value_part = jnp.dot(scaled, w_value, preferred_element_type=jnp.float32)]
  transfers between devices with their start and end apart: 3 -> 5, of which waited for: 2 -> 2; matrix products, arithmetic and copies ran while one was open for 2% -> 9% of each run, Pallas kernels for 0% -> 0%
where the time goes in v1:
time: 149 us
  blocking collectives  63.8 us (43%)
  waiting for transfers between devices  31.4 us (21%)
  matrix products  21.3 us (14%)
  between operations  14.3 us (10%)
  starting transfers between devices  8.29 us (6%)
  local copies, waits for them, and re-layouts  5.77 us (4%)
  other arithmetic  4.09 us (3%)
    psum x1, waiting for transfers between devices, local(): lax.psum((query_part, key_part, value_part), 'seq')  30.4 us
    all_gather x2, blocking collectives, joined(): pieces = jax.tree.map(lambda part: lax.all_gather(part, axis), value)  22.4 us
    unnamed x1, blocking collectives  18.1 us
    psum x1, blocking collectives, local(): lax.psum((query_part, key_part, value_part), 'seq')  16.3 us
    dot_general x1, matrix products, local(): query_part = jnp.dot(scaled, w_query, preferred_element_type=jnp.float32)  9.65 us
    dot_general x1, matrix products, local(): jnp.dot(mixed, w_out, preferred_element_type=jnp.float32)  7.7 us
    all_gather x1, blocking collectives, local(): token_rows = lax.all_gather(hidden, 'head', axis=0, tiled=True)  7.05 us
    unnamed x1, starting transfers between devices  4.3 us
  transfers between devices with their start and end apart: 5, of which 2 were waited for; matrix products, arithmetic and copies ran while one was open for 9% of the time, Pallas kernels for 0%

profile of v1, /device:TPU:1, one launch (start us, length us, event | category | flops | bytes accessed | tf_op | source)
XLA Modules:
  0.0 149.0 jit_solution(6374439148872609451)
XLA Ops:
  6.5 7.0 %all-gather.3 = bf16[4,6,3072]{2,1,0:T(8,128)(2,1)S(1)} all-gather(bf16[1,6,3072]{2,1,0:T(8,128)(2,1)} %bitcast.49), channel_id=1, replica_groups=mesh['parts'=2,'seq'=4,'head'=4] {'head'}, dimensions={0}, use_global_device_ids=true | all-gather | bytes 184320 | tf_op jit(solution)/shard_map/all_gather | solution.py:42
  13.6 0.9 multiply_reduce_fusion
  14.5 1.6 %collective-permute-start = (f32[24]{0:T(128)S(1)}, f32[24]{0:T(128)S(1)}, u32[]{:S(2)}, u32[]{:S(2)}) collective-permute-start(f32[24]{0:T(128)S(1)} %get-tuple-element.84), channel_id=1, source_target_pairs={{0,4},{4,0},{8,12},{12,8},{1,5},{5,1},{9,13},{13,9},{2,6},{6,2},{1... | collective-permute-start | bytes 296 | tf_op jit(solution)/shard_map/ppermute | solution.py:15
  16.1 9.7 %fusion.12 = f32[24,3072]{1,0:T(8,128)} fusion(bf16[24,3072]{1,0:T(8,128)(2,1)S(1)} %get-tuple-element.85, bf16[3072,3072]{1,0:T(8,128)(2,1)} %param.13), kind=kOutput, calls=%fused_computation.30 | convolution fusion | flops 452984832 | bytes 19316736 | tf_op jit(solution)/shard_map/dot_general | solution.py:46
  25.8 2.4 %collective-permute-start.1 = (f32[24]{0:T(128)S(1)}, f32[24]{0:T(128)S(1)}, u32[]{:S(2)}, u32[]{:S(2)}) collective-permute-start(f32[24]{0:T(128)S(1)} %add.44), channel_id=1, source_target_pairs={{0,8},{4,12},{8,0},{12,4},{1,9},{5,13},{9,1},{13,5},{2,10},{6,14},... | collective-permute-start | bytes 296 | tf_op jit(solution)/shard_map/ppermute | solution.py:15
  28.3 0.9 collective-permute-done.1
  29.2 30.4 %all-reduce.5.cloned.1.call-done = f32[24,3072]{1,0:T(8,128)} async-done(((f32[24,3072]{1,0:T(8,128)}), f32[24,3072]{1,0:T(8,128)}) %all-reduce.5.cloned.1.call-update) | async-done | bytes 294928 | tf_op jit(solution)/shard_map/psum | solution.py:51
  59.6 1.1 multiply_convert_fusion
  60.8 1.0 select_reduce_fusion
  61.8 0.4 copy-done.4
  62.2 0.6 fusion.8
  62.8 0.9 copy.26
  63.8 1.8 %fusion.15 = f32[24,256]{1,0:T(8,128)S(1)} fusion(bf16[24,3072]{1,0:T(8,128)(2,1)S(1)} %get-tuple-element.85, bf16[3072,256]{1,0:T(8,128)(2,1)} %param.15), kind=kOutput, calls=%fused_computation.33 | convolution fusion | flops 37748736 | bytes 1744896 | tf_op jit(solution)/shard_map/dot_general | solution.py:48
  66.0 16.3 %all-reduce.2 = (f32[24,256]{1,0:T(8,128)S(1)}, f32[24,256]{1,0:T(8,128)S(1)}) all-reduce(f32[24,256]{1,0:T(8,128)S(1)} %fusion.13, f32[24,256]{1,0:T(8,128)S(1)} %fusion.15), channel_id=1, replica_groups=mesh['parts'=2,'seq'=4,'head'=4] {'seq'}, use_global_device_ids=true, to_apply=%region_6.7 | all-reduce | flops 12288 | bytes 98304 | tf_op jit(solution)/shard_map/psum | solution.py:51
  82.3 12.0 %all-gather = f32[96,2,12]{2,1,0:T(2,128)S(1)} all-gather(f32[24,2,12]{2,1,0:T(2,128)S(1)} %get-tuple-element.88), channel_id=2, replica_groups=mesh['parts'=2,'seq'=4,'head'=4] {'seq'}, dimensions={0}, use_global_device_ids=true | all-gather | bytes 11520 | tf_op jit(solution)/shard_map/all_gather | solution.py:23
  94.7 10.4 %all-gather.1 = f32[96,2,12]{2,1,0:T(2,128)S(1)} all-gather(f32[24,2,12]{2,1,0:T(2,128)S(1)} %convert_reduce_fusion), channel_id=3, replica_groups=mesh['parts'=2,'seq'=4,'head'=4] {'seq'}, dimensions={0}, use_global_device_ids=true | all-gather | bytes 11520 | tf_op jit(solution)/shard_map/all_gather | solution.py:23
  105.9 1.1 slice.32
  107.1 2.0 %while.14 = (s32[]{:T(128)}, f32[24,2,12]{0,1,2:T(2,128)S(1)}, f32[24,2,12]{0,1,2:T(2,128)S(1)}, f32[24,2,12,128]{3,2,1,0:T(8,128)S(1)}, f32[3,24,2,12]{1,2,3,0:...) while((s32[]{:T(128)}, f32[24,2,12]{0,1,2:T(2,128)S(1)}, ...), condition=%wide.region_5.6_spmd, body=%wide.region_4.5_spmd.sunk | while | flops 224642 | bytes 1506917 | solution.py:26
  107.4 0.4 fusion.33
  109.9 7.7 %fusion.16 = f32[24,3072]{1,0:T(8,128)S(1)} fusion(bf16[24,3072]{1,0:T(8,128)(2,1)S(1)} %reshape.56, bf16[3072,3072]{1,0:T(8,128)(2,1)} %param.16), kind=kOutput, calls=%fused_computation.34 | convolution fusion | flops 452984832 | bytes 19316736 | tf_op jit(solution)/shard_map/dot_general | solution.py:92
  117.6 18.1 %fusion = f32[8,3072]{1,0:T(8,128)S(1)} fusion(f32[24,3072]{1,0:T(8,128)S(1)} %fusion.16), kind=kCustom, calls=%all-reduce-scatter | all-reduce-scatter fusion | flops 98305 | bytes 393728
  135.8 4.3 %collective-permute-start.2 = (bf16[6,3072]{1,0:T(8,128)(2,1)S(1)}, bf16[6,3072]{1,0:T(8,128)(2,1)S(1)}, u32[]{:S(2)}, u32[]{:S(2)}) collective-permute-start(bf16[6,3072]{1,0:T(8,128)(2,1)S(1)} %slice.36), channel_id=1, source_target_pairs={{0,1},{1,2},{2,3},{4,5},{5,6},{6,7},{8,9},{9,10},{10,11},{12,13},{... | collective-permute-start | bytes 110600
  140.1 0.6 dynamic-slice.4
  141.6 0.6 dynamic-slice_convert_fusion
  (62 shorter events, 4.6 us)
Async XLA Ops:
  6.5 54.3 %copy-start = (bf16[24,2,128,128]{3,2,1,0:T(8,128)(2,1)S(1)}, bf16[24,2,128,128]{3,2,1,0:T(8,128)(2,1)}, u32[]{:S(2)}) copy-start(bf16[24,2,128,128]{3,2,1,0:T(8,128)(2,1)} %param.18) | copy-start | bytes 4718596
  6.5 53.1 %all-reduce.5.cloned.1.call-start = ((), (), s32[]{:S(2)}) async-start(), calls=%async_computation | async-start | bytes 589824 | tf_op jit(solution)/shard_map/psum | solution.py:51
  14.5 11.3 %collective-permute-start = (f32[24]{0:T(128)S(1)}, f32[24]{0:T(128)S(1)}, u32[]{:S(2)}, u32[]{:S(2)}) collective-permute-start(f32[24]{0:T(128)S(1)} %get-tuple-element.84), channel_id=1, source_target_pairs={{0,4},{4,0},{8,12},{12,8},{1,5},{5,1},{9,13},{13,9},{2,6},{6,2},{1... | collective-permute-start | bytes 296 | tf_op jit(solution)/shard_map/ppermute | solution.py:15
  16.1 12.1 %copy-start.3 = (s32[24]{0:T(128)S(1)}, s32[24]{0:T(128)}, u32[]{:S(2)}) copy-start(s32[24]{0:T(128)} %param.17) | copy-start | bytes 292
  25.7 80.1 %all-gather.6.cloned.1.call-start = ((), (), s32[]{:S(2)}) async-start(), calls=%async_computation.1 | async-start | bytes 1474560 | tf_op jit(solution)/shard_map/all_gather | solution.py:23
  25.8 3.4 %collective-permute-start.1 = (f32[24]{0:T(128)S(1)}, f32[24]{0:T(128)S(1)}, u32[]{:S(2)}, u32[]{:S(2)}) collective-permute-start(f32[24]{0:T(128)S(1)} %add.44), channel_id=1, source_target_pairs={{0,8},{4,12},{8,0},{12,4},{1,9},{5,13},{9,1},{13,5},{2,10},{6,14},... | collective-permute-start | bytes 296 | tf_op jit(solution)/shard_map/ppermute | solution.py:15
  60.8 1.4 copy-start.4
  63.7 1.9 %copy-start.1 = (bf16[3072,256]{1,0:T(8,128)(2,1)S(1)}, bf16[3072,256]{1,0:T(8,128)(2,1)}, u32[]{:S(2)}) copy-start(bf16[3072,256]{1,0:T(8,128)(2,1)} %param.14) | copy-start | bytes 4718596
  105.9 1.3 slice-start
  109.9 30.2 %copy-start.2 = (u32[32]{0:T(128)S(1)}, u32[32]{0:T(128)}, u32[]{:S(2)}) copy-start(u32[32]{0:T(128)} %constant.37) | copy-start | bytes 388
  135.8 5.6 %collective-permute-start.2 = (bf16[6,3072]{1,0:T(8,128)(2,1)S(1)}, bf16[6,3072]{1,0:T(8,128)(2,1)S(1)}, u32[]{:S(2)}, u32[]{:S(2)}) collective-permute-start(bf16[6,3072]{1,0:T(8,128)(2,1)S(1)} %slice.36), channel_id=1, source_target_pairs={{0,1},{1,2},{2,3},{4,5},{5,6},{6,7},{8,9},{9,10},{10,11},{12,13},{... | collective-permute-start | bytes 110600
Sparse Core Ops, SparseCore 0:
  25.9 33.7 all-reduce.4
  63.9 33.6 all-gather.5
